TPU v7x, 32 devices: a whole 2x2x4 slice. The times are simulated.
32 devices in a mesh: space: 2 (over y), chaos: 16 (over z, x, core).
Axes of the slice: x: 2, y: 2, z: 4, core: 2. Of those that a mesh axis runs over, the one named last changes fastest.
Arguments:
- kl_fields: float32 [9, 4, 16, 512], P(None, None, 'space'), may hold values from -5 to 5
- labels: int32 [4, 16, 512], P(None, 'space'), may hold values from 0 to 3
- region_scale: float32 [4, 9], replicated, may hold values from 0.5 to 2
- background: float32 [4, 16, 512], P(None, 'space'), may hold values from -4 to 4
- galerkin_table: int32 [384, 3], replicated, may hold values from 0 to 47, as said below
- triple_values: float32 [384], replicated, may hold values from -4 to 4
- direction: float32 [48, 3, 4, 16, 512], P('chaos', None, None, 'space'), may hold values from -6 to 6
Outputs:
- result: float32 [48, 3, 4, 16, 512], P('chaos', None, None, 'space')
Inputs may be any that keep to these rules, and one draw needn't show every extreme that they name: `galerkin_table`: row r has term i = r // 8; the first row of each term is (i, i, 0); the others name any term j and a mode k of 1 to 8.
All inputs are finite; a program needn't handle non-finite values.
Results may differ from a plain program's by a relative error of at most 0.000076.
Values sent between devices are 32-bit elements; how exact they have to be, the bound alone decides.
A program may use at most 128 MiB of HBM per device.

v0:
```python
import jax
import jax.numpy as jnp
from jax import lax
from jax.sharding import PartitionSpec as P


def extended(array, sides, width):
    for axis, dim in sides:
        size, length = (lax.axis_size(axis), array.shape[dim])
        up = [(i, (i + 1) % size) for i in range(size - 1)]
        down = [(j, i) for i, j in up]
        last = lax.slice_in_dim(array, length - width, length, axis=dim)
        initial = lax.slice_in_dim(array, 0, width, axis=dim)
        before = lax.ppermute(last, axis, up)
        after = lax.ppermute(initial, axis, down)
        array = jnp.concatenate([before, array, after], axis=dim)
    return array


def neighbours(padded):
    middle = padded[..., 1:-1, :]
    row_next = padded[..., 2:, :]
    row_prev = padded[..., :-2, :]
    plane_zero = jnp.zeros_like(middle[..., :1, :, :])
    plane_next = jnp.concatenate([middle[..., 1:, :, :], plane_zero], axis=-3)
    plane_prev = jnp.concatenate([plane_zero, middle[..., :-1, :, :]], axis=-3)
    column_zero = jnp.zeros_like(middle[..., :1])
    column_next = jnp.concatenate([middle[..., 1:], column_zero], axis=-1)
    column_prev = jnp.concatenate([column_zero, middle[..., :-1]], axis=-1)
    return (middle, (row_next, row_prev, plane_next, plane_prev, column_next, column_prev))


def drift_terms(potential_pad):
    middle, beside_all = neighbours(potential_pad)
    return tuple((0.5 * (other - middle) for other in beside_all))


def jacobian_block(coef_pad, potential_pad, electron_pad, hole_pad, drift_list):
    coef_mid, coef_nbr = neighbours(coef_pad)
    pot_mid, pot_nbr = neighbours(potential_pad)
    ele_mid, ele_nbr = neighbours(electron_pad)
    hole_mid, hole_nbr = neighbours(hole_pad)
    out_potential = coef_mid * (ele_mid - hole_mid)
    out_electron = jnp.zeros_like(out_potential)
    out_holes = jnp.zeros_like(out_potential)
    for facing in range(6):
        conduct = 0.5 * (coef_mid + coef_nbr[facing])
        potential_rise = pot_nbr[facing] - pot_mid
        drift_now = drift_list[facing]
        out_potential = out_potential - conduct * potential_rise
        out_electron = out_electron + conduct * (
            ele_mid - ele_nbr[facing] - drift_now * (ele_mid + ele_nbr[facing]) - potential_rise
        )
        out_holes = out_holes + conduct * (
            hole_mid - hole_nbr[facing] + drift_now * (hole_mid + hole_nbr[facing]) + potential_rise
        )
    return jnp.stack([out_potential, out_electron, out_holes], axis=-4)


def shards(kl_fields, labels, region_scale, background, galerkin_table, triple_values, direction):
    term_dev = direction.shape[0]
    group_count = lax.axis_size("chaos")
    all_terms = term_dev * group_count
    first_term = lax.axis_index("chaos") * term_dev
    region_count = region_scale.shape[0]
    mode_count = region_scale.shape[1]
    lookup = jnp.zeros(kl_fields.shape, jnp.float32)
    for region in range(region_count):
        lookup = (
            lookup
            + (labels == region).astype(jnp.float32)[None]
            * region_scale[region][:, None, None, None]
        )
    scaled = kl_fields * lookup
    stacked = jnp.concatenate([scaled, background[None]], axis=0)
    rimmed = extended(stacked, (("space", 2),), 1)
    coef_pad = rimmed[:-1]
    drift_list = drift_terms(rimmed[-1])
    local_hot = (
        galerkin_table[:, 0][:, None] == first_term + jnp.arange(term_dev, dtype=jnp.int32)[None]
    ).astype(jnp.float32)
    source_hot = (
        galerkin_table[:, 1][:, None] == jnp.arange(all_terms, dtype=jnp.int32)[None]
    ).astype(jnp.float32)
    mode_hot = (
        galerkin_table[:, 2][:, None] == jnp.arange(mode_count, dtype=jnp.int32)[None]
    ).astype(jnp.float32)
    mixing = jnp.einsum(
        "t,ta,tj,tk->ajk",
        triple_values,
        local_hot,
        source_hot,
        mode_hot,
        precision=lax.Precision.HIGHEST,
    )
    zeros_out = jnp.zeros(direction.shape, jnp.float32)
    own_pad = extended(direction, (("space", 3),), 1)
    term_block = lax.all_gather(own_pad, "chaos", axis=0, tiled=True)
    block_terms = term_block.shape[0]

    def one_pair(pair_index, total):
        target = pair_index // block_terms
        source = pair_index % block_terms
        pair_weights = mixing[target, source]

        def apply_pair(unused):
            pair_coef = jnp.einsum(
                "k,kprc->prc", pair_weights, coef_pad, precision=lax.Precision.HIGHEST
            )
            fields = lax.dynamic_index_in_dim(term_block, source, 0, keepdims=False)
            return jacobian_block(pair_coef, fields[0], fields[1], fields[2], drift_list)

        def skip_pair(unused):
            return jnp.zeros(direction.shape[1:], jnp.float32)

        update = lax.cond(jnp.any(pair_weights != 0.0), apply_pair, skip_pair, 0)
        current = lax.dynamic_index_in_dim(total, target, 0, keepdims=False)
        return lax.dynamic_update_index_in_dim(total, current + update, target, 0)

    return lax.fori_loop(0, term_dev * block_terms, one_pair, zeros_out)


def solution(mesh):
    return jax.shard_map(
        shards,
        mesh=mesh,
        in_specs=(
            P(None, None, "space", None),
            P(None, "space", None),
            P(),
            P(None, "space", None),
            P(),
            P(),
            P("chaos", None, None, "space", None),
        ),
        out_specs=P("chaos", None, None, "space", None),
        check_vma=False,
    )
```

profile of v0, /device:TPU:2, one launch (start us, length us, event | category | flops | bytes accessed | tf_op | source)
XLA Modules:
  0.0 423.2 jit_solution(8876589187335992419)
XLA Ops:
  6.5 1.4 copy.9
  8.0 3.6 collective-permute-start.2
  11.6 1.3 collective-permute-start.3
  13.6 4.3 %collective-permute-done.3 = f32[3,3,4,1,512]{4,2,3,1,0:T(4,128)S(1)} collective-permute-done((f32[3,3,4,1,512]{4,2,3,1,0:T(4,128)S(1)}, f32[3,3,4,1,512]{4,2,3,1,0:T(4,128)S(1)}, u32[]{:S(2)}, u32[]{:S(2)}) %collective-permute-start.3) | collective-permute-done | bytes 73760 | tf_op jit(solution)/shard_map/ppermute | solution.py:15
  19.9 1.6 collective-permute-start
  21.5 1.3 collective-permute-start.1
  23.5 4.3 %collective-permute-done.1 = f32[10,4,1,512]{3,2,1,0:T(1,128)S(1)} collective-permute-done((f32[10,4,1,512]{3,2,1,0:T(1,128)S(1)}, f32[10,4,1,512]{3,2,1,0:T(1,128)S(1)}, u32[]{:S(2)}, u32[]{:S(2)}) %collective-permute-start.1) | collective-permute-done | bytes 81952 | tf_op jit(solution)/shard_map/ppermute | solution.py:15
  28.4 85.6 %all-gather.2.cloned.1.call-done = f32[48,3,4,10,512]{4,2,3,1,0:T(4,128)} async-done(((f32[3,3,4,10,512]{4,2,3,1,0:T(4,128)}), f32[48,3,4,10,512]{4,2,3,1,0:T(4,128)}) %all-gather.2.cloned.1.call-update) | async-done | bytes 11796496 | tf_op jit(solution)/shard_map/all_gather | solution.py:98
  114.1 17.0 %copy.13 = f32[48,3,4,10,512]{4,3,2,1,0:T(8,128)} copy(f32[48,3,4,10,512]{4,2,3,1,0:T(4,128)} %all-gather.2.cloned.1.call-done) | data formatting | bytes 23592960 | tf_op jit(solution)/shard_map/while | solution.py:120
  131.1 284.4 %while.15 = (s32[]{:T(128)}, f32[3,3,4,8,512]{4,3,2,1,0:T(8,128)S(1)}, f32[3,48,9]{2,1,0:T(8,128)S(1)}, f32[9,4,10,512]{3,2,1,0:T(8,128)S(1)}, f32[48,3,4,10,512...) while((s32[]{:T(128)}, ...), condition=%wide.region_4.5_spmd, body=%wide.region_0.4_spmd.sunk | while | flops 4816939 | bytes 9204332 | solution.py:120
  132.5 3.1 conditional.2
  144.3 3.1 conditional.2
  145.6 1.1 fusion
  153.2 3.1 conditional.2
  165.1 3.1 conditional.2
  169.6 3.1 conditional.2
  170.8 1.1 fusion
  190.3 3.1 conditional.2
  191.5 1.1 fusion
  203.6 3.1 conditional.2
  204.8 1.1 fusion
  222.8 3.1 conditional.2
  224.0 1.1 fusion
  227.3 3.1 conditional.2
  228.5 1.1 fusion
  237.7 3.1 conditional.2
  238.9 1.1 fusion
  243.6 3.1 conditional.2
  244.9 1.1 fusion
  252.5 3.1 conditional.2
  253.8 1.1 fusion
  280.6 3.1 conditional.2
  281.8 1.1 fusion
  286.5 3.1 conditional.2
  292.5 3.1 conditional.2
  293.7 1.1 fusion
  308.8 3.1 conditional.2
  310.0 1.1 fusion
  326.5 3.1 conditional.2
  331.0 3.1 conditional.2
  332.2 1.1 fusion
  338.4 3.1 conditional.2
  339.7 1.1 fusion
  342.9 3.1 conditional.2
  353.3 3.1 conditional.2
  374.0 3.1 conditional.2
  388.8 3.1 conditional.2
  400.6 3.1 conditional.2
  (959 shorter events, 170.3 us)
Async XLA Ops:
  6.5 107.5 %all-gather.2.cloned.1.call-start = ((), (), s32[]{:S(2)}) async-start(), calls=%async_computation | async-start | bytes 12533760 | tf_op jit(solution)/shard_map/all_gather | solution.py:98
  8.0 11.0 %copy-start.5 = (f32[4,9]{1,0:T(4,128)S(1)}, f32[4,9]{1,0:T(4,128)}, u32[]{:S(2)}) copy-start(f32[4,9]{1,0:T(4,128)} %param.13) | copy-start | bytes 436
  8.0 11.0 %copy-start.3 = (s32[4,8,512]{2,1,0:T(8,128)S(1)}, s32[4,8,512]{2,1,0:T(8,128)}, u32[]{:S(2)}) copy-start(s32[4,8,512]{2,1,0:T(8,128)} %param.12) | copy-start | bytes 196612
  8.0 11.0 %copy-start.1 = (f32[9,4,8,512]{3,2,1,0:T(8,128)S(1)}, f32[9,4,8,512]{3,2,1,0:T(8,128)}, u32[]{:S(2)}) copy-start(f32[9,4,8,512]{3,2,1,0:T(8,128)} %param.11) | copy-start | bytes 1769476
  8.0 5.5 %collective-permute-start.2 = (f32[3,3,4,1,512]{4,2,3,1,0:T(4,128)S(1)}, f32[3,3,4,1,512]{4,2,3,1,0:T(4,128)S(1)}, u32[]{:S(2)}, u32[]{:S(2)}) collective-permute-start(f32[3,3,4,1,512]{4,2,3,1,0:T(4,128)S(1)} %get-tuple-element.391), channel_id=1, source_target_pairs={{0,16},{1,17},{2,18},{3,19},{4,20},{5,21},{6,22},{7,23},{8,24},{9,... | collective-permute-start | bytes 221192 | tf_op jit(solution)/shard_map/ppermute | solution.py:14
  11.6 6.2 %collective-permute-start.3 = (f32[3,3,4,1,512]{4,2,3,1,0:T(4,128)S(1)}, f32[3,3,4,1,512]{4,2,3,1,0:T(4,128)S(1)}, u32[]{:S(2)}, u32[]{:S(2)}) collective-permute-start(f32[3,3,4,1,512]{4,2,3,1,0:T(4,128)S(1)} %get-tuple-element.392), channel_id=1, source_target_pairs={{16,0},{17,1},{18,2},{19,3},{20,4},{21,5},{22,6},{23,7},{24,8},{25... | collective-permute-start | bytes 221192 | tf_op jit(solution)/shard_map/ppermute | solution.py:15
  18.9 0.8 copy-start.2
  19.0 3.8 copy-start.4
  19.0 3.8 copy-start.6
  19.9 3.6 collective-permute-start
  21.5 6.3 %collective-permute-start.1 = (f32[10,4,1,512]{3,2,1,0:T(1,128)S(1)}, f32[10,4,1,512]{3,2,1,0:T(1,128)S(1)}, u32[]{:S(2)}, u32[]{:S(2)}) collective-permute-start(f32[10,4,1,512]{3,2,1,0:T(1,128)S(1)} %get-tuple-element.390), channel_id=1, source_target_pairs={{16,0},{17,1},{18,2},{19,3},{20,4},{21,5},{22,6},{23,7},{24,8},{25... | collective-permute-start | bytes 245768 | tf_op jit(solution)/shard_map/ppermute | solution.py:15
  415.5 0.8 copy-start
Sparse Core Ops, SparseCore 0:
  19.1 94.9 all-gather.1
where the time goes:
time: 425 us; the launch traced here: 423 us
  other arithmetic  115 us (27%)
  loops' own time  107 us (25%)
  waiting for transfers between devices  95.2 us (22%)
  local copies, waits for them, and re-layouts  57 us (13%)
  matrix products  27.5 us (6%)
  between operations  13.6 us (3%)
  starting transfers between devices  7.71 us (2%)
    another operation x1, loops' own time, shards(): return lax.fori_loop(0, term_dev * block_terms, one_pair, zeros_out)  102 us
    reduce_or x144, other arithmetic, one_pair(): update = lax.cond(jnp.any(pair_weights != 0.0), apply_pair, skip_pair, 0)  96.1 us
    all_gather x1, waiting for transfers between devices, shards(): term_block = lax.all_gather(own_pad, 'chaos', axis=0, tiled=True)  85.6 us
    dot_general x24, matrix products, apply_pair(): jnp.einsum('k,kprc->prc', pair_weights, coef_pad, precision=lax.Precision...  27.4 us
    squeeze x24, local copies, waits for them, and re-layouts, apply_pair(): fields[1]  25.6 us
    while x2, local copies, waits for them, and re-layouts, shards(): return lax.fori_loop(0, term_dev * block_terms, one_pair, zeros_out)  17.1 us
    another operation x96, other arithmetic, jacobian_block(): return jnp.stack([out_potential, out_electron, out_holes], axis=-4)  11.9 us
    ppermute x2, waiting for transfers between devices, extended(): after = lax.ppermute(initial, axis, down)  8.58 us
  transfers between devices with their start and end apart: 5, of which 5 were waited for; matrix products, arithmetic and copies ran while one was open for 0% of the time, Pallas kernels for 0%

commit v1 on v0

v1 whole, which is shorter than its diff:
```python
import functools

import jax
import jax.numpy as jnp
from jax import lax
from jax.experimental import pallas as pl
from jax.experimental.pallas import tpu as pltpu
from jax.sharding import PartitionSpec as P

MESH = pl.DeviceIdType.MESH
FACES = 6


def offset_of(step, group):
    sign = 1 - 2 * (step % 2)
    return group // 2 + sign * ((step + 1) // 2)


def kernel(
    dims,
    kl,
    labels,
    background,
    direction,
    scale,
    table,
    values,
    out,
    send,
    recv,
    result,
    back,
    kl_tiles,
    label_tiles,
    coef,
    coef_halo,
    halo,
    conduct,
    drift,
    flux,
    send_sem,
    recv_sem,
    back_send_sem,
    back_recv_sem,
    row_send_sem,
    row_recv_sem,
):
    group, space, terms, fields, planes, width, modes, regions, per_term = dims
    count = terms * fields
    rows = direction.shape[2]
    lanes = planes * width
    blocks = lanes // width
    chunks = group // blocks
    me = lax.axis_index("chaos")
    here = lax.axis_index("space")

    lane = lax.broadcasted_iota(jnp.int32, (rows, lanes), 1)
    row = lax.broadcasted_iota(jnp.int32, (rows, lanes), 0)
    column = lane % width
    plane = lane // width

    barrier = pltpu.get_barrier_semaphore()
    for g in range(1, group):
        pl.semaphore_signal(
            barrier, inc=1, device_id={"chaos": lax.rem(me + g, group)}, device_id_type=MESH
        )

    @pl.when(here > 0)
    def _():
        pl.semaphore_signal(barrier, inc=1, device_id={"space": here - 1}, device_id_type=MESH)

    @pl.when(here < space - 1)
    def _():
        pl.semaphore_signal(barrier, inc=1, device_id={"space": here + 1}, device_id_type=MESH)

    def turn(tile, shift, axis=1):
        shift = shift % tile.shape[axis]
        return tile if shift == 0 else pltpu.roll(tile, shift, axis)

    def swap_blocks(tiles):
        swapped = []
        for m in range(blocks):
            tile = tiles[0] if m == 0 else turn(tiles[0], -width * m)
            for p in range(1, blocks):
                tile = jnp.where(plane == p, turn(tiles[p], width * (p - m)), tile)
            swapped.append(tile)
        return swapped

    @pl.loop(0, count)
    def _(n):
        for q in range(chunks):
            part = [direction[n, p, :, lanes * q : lanes * (q + 1)] for p in range(planes)]
            for m, tile in enumerate(swap_blocks(part)):
                send[blocks * q + m, n] = tile

    half = width // 2

    @pl.loop(0, group)
    def _(d):
        after = jnp.minimum(d + 1, group - 1)
        before = jnp.maximum(d - 1, 0)
        right = jnp.zeros((rows, lanes), jnp.float32)
        left = jnp.zeros((rows, lanes), jnp.float32)
        for n in range(count):
            right = jnp.where(column == n, turn(send[after, n], n), right)
            left = jnp.where(column == half + n, turn(send[before, n], half + n - (width - 1)), left)
        right = jnp.where(d < group - 1, right, 0.0)
        left = jnp.where(d > 0, left, 0.0)
        send[d, count] = jnp.where(column < half, right, left)

    beside = jnp.minimum(here, 1) + jnp.minimum(space - 1 - here, 1)
    pl.semaphore_wait(barrier, group - 1 + beside)

    def forth(source, target):
        return pltpu.make_async_remote_copy(
            src_ref=send.at[target],
            dst_ref=recv.at[source],
            send_sem=send_sem.at[target],
            recv_sem=recv_sem.at[source],
            device_id={"chaos": target},
            device_id_type=MESH,
        )

    @pl.loop(0, group - 1)
    def _(step):
        forth(me, lax.rem(me + offset_of(step, group), group)).start()

    @pl.loop(0, count + 1)
    def _(n):
        recv[me, n] = send[me, n]

    @pl.loop(0, modes)
    def _(k):
        for q in range(chunks):
            part = [kl[k, p, :, lanes * q : lanes * (q + 1)] for p in range(planes)]
            for m, tile in enumerate(swap_blocks(part)):
                kl_tiles[blocks * q + m, k] = tile

    for q in range(chunks):
        part = [background[p, :, lanes * q : lanes * (q + 1)] for p in range(planes)]
        for m, tile in enumerate(swap_blocks(part)):
            kl_tiles[blocks * q + m, modes] = tile
        part = [labels[p, :, lanes * q : lanes * (q + 1)] for p in range(planes)]
        for m, tile in enumerate(swap_blocks(part)):
            label_tiles[blocks * q + m] = tile

    places = (me, jnp.minimum(me + 1, group - 1), jnp.maximum(me - 1, 0))
    inside = (None, me < group - 1, me > 0)
    for slot, (place, ok) in enumerate(zip(places, inside)):
        region_tile = label_tiles[place]
        for k in range(modes):
            lookup = jnp.full((rows, lanes), scale[0, k])
            for region in range(1, regions):
                lookup = jnp.where(region_tile == region, scale[region, k], lookup)
            tile = kl_tiles[place, k] * lookup
            coef[slot, k] = tile if ok is None else jnp.where(ok, tile, 0.0)
        tile = kl_tiles[place, modes]
        coef[slot, modes] = tile if ok is None else jnp.where(ok, tile, 0.0)


    def row_copy(part, way):
        buffer = (coef_halo, halo)[part]
        return pltpu.make_async_remote_copy(
            src_ref=buffer.at[way],
            dst_ref=buffer.at[2 + way],
            send_sem=row_send_sem.at[part, way],
            recv_sem=row_recv_sem.at[part, way],
            device_id={"space": here + (1 if way == 0 else -1)},
            device_id_type=MESH,
        )

    def start_rows(part):
        @pl.when(here < space - 1)
        def _():
            row_copy(part, 0).start()

        @pl.when(here > 0)
        def _():
            row_copy(part, 1).start()

    def finish_rows(part):
        buffer = (coef_halo, halo)[part]

        @pl.when(here > 0)
        def _():
            row_copy(part, 0).wait_recv()

        @pl.when(here < space - 1)
        def _():
            row_copy(part, 1).wait_recv()

        @pl.when(here == 0)
        def _():
            buffer[2] = jnp.zeros(buffer.shape[1:], jnp.float32)

        @pl.when(here == space - 1)
        def _():
            buffer[3] = jnp.zeros(buffer.shape[1:], jnp.float32)

        @pl.when(here < space - 1)
        def _():
            row_copy(part, 0).wait_send()

        @pl.when(here > 0)
        def _():
            row_copy(part, 1).wait_send()

    for k in range(modes + 1):
        coef_halo[0, k] = coef[0, k, rows - 1 : rows, :]
        coef_halo[1, k] = coef[0, k, 0:1, :]

    def side_neighbours(tile, after, before):
        return (
            jnp.where(plane < planes - 1, turn(tile, -width), 0.0),
            jnp.where(plane > 0, turn(tile, width), 0.0),
            jnp.where(column == width - 1, after, turn(tile, -1)),
            jnp.where(column == 0, before, turn(tile, 1)),
        )

    def row_neighbours(tile, above, below):
        return (
            jnp.where(row == rows - 1, jnp.broadcast_to(below, tile.shape), turn(tile, -1, 0)),
            jnp.where(row == 0, jnp.broadcast_to(above, tile.shape), turn(tile, 1, 0)),
        )

    start_rows(0)

    for k in range(modes + 1):
        tile = coef[0, k]
        others = side_neighbours(
            tile, turn(coef[1, k], width - 1), turn(coef[2, k], 1 - width)
        )
        for face, other in enumerate(others):
            if k < modes:
                conduct[k, 2 + face] = 0.5 * (tile + other)
            else:
                drift[2 + face] = 0.5 * (other - tile)
        if k < modes:
            conduct[k, FACES] = tile

    finish_rows(0)
    for k in range(modes + 1):
        tile = coef[0, k]
        for face, other in enumerate(row_neighbours(tile, coef_halo[2, k], coef_halo[3, k])):
            if k < modes:
                conduct[k, face] = 0.5 * (tile + other)
            else:
                drift[face] = 0.5 * (other - tile)

    def store_flux(j, face, tiles, others):
        slope = drift[face]
        (u, v, w), (un, vn, wn) = tiles, others
        rise = un - u
        flux[j, 3 * face] = -rise
        flux[j, 3 * face + 1] = (v - vn) - slope * (v + vn) - rise
        flux[j, 3 * face + 2] = (w - wn) + slope * (w + wn) + rise

    @pl.loop(0, group)
    def _(step):
        source = lax.rem(me + group - offset_of(group - 1 - step, group), group)

        @pl.when(step > 0)
        def _():
            forth(source, source).wait_recv()

        rim = recv[source, count]
        for t in range(terms):
            j = source * terms + t
            tiles = [recv[source, t * fields + f] for f in range(fields)]
            others = []
            for f in range(fields):
                n = t * fields + f
                halo[0, source * count + n] = tiles[f][rows - 1 : rows]
                halo[1, source * count + n] = tiles[f][0:1]
                others.append(
                    side_neighbours(
                        tiles[f], turn(rim, width - 1 - n), turn(rim, -half - n)
                    )
                )
            for face in range(4):
                store_flux(j, 2 + face, tiles, [o[face] for o in others])
            flux[j, 3 * FACES] = tiles[1] - tiles[2]

    start_rows(1)
    finish_rows(1)

    @pl.loop(0, group)
    def _(source):
        for t in range(terms):
            j = source * terms + t
            tiles = [recv[source, t * fields + f] for f in range(fields)]
            others = [
                row_neighbours(
                    tiles[f],
                    halo[2, source * count + t * fields + f],
                    halo[3, source * count + t * fields + f],
                )
                for f in range(fields)
            ]
            for face in range(2):
                store_flux(j, face, tiles, [o[face] for o in others])

    def home(source, target):
        return pltpu.make_async_remote_copy(
            src_ref=result.at[target],
            dst_ref=back.at[source],
            send_sem=back_send_sem.at[target],
            recv_sem=back_recv_sem.at[source],
            device_id={"chaos": target},
            device_id_type=MESH,
        )

    @pl.loop(0, group)
    def _(step):
        target = lax.rem(me + offset_of(step, group), group)
        for t in range(terms):
            total = [jnp.zeros((rows, lanes), jnp.float32) for _ in range(fields)]
            for e in range(per_term):
                entry = (target * terms + t) * per_term + e
                j, k, value = table[0, entry], table[1, entry], values[entry]
                total[0] += (value * conduct[k, FACES]) * flux[j, 3 * FACES]
                for face in range(FACES):
                    h = value * conduct[k, face]
                    for f in range(fields):
                        total[f] += h * flux[j, 3 * face + f]
            for f in range(fields):
                result[target, t * fields + f] = total[f]

        @pl.when(step > 0)
        def _():
            home(me, lax.rem(me + offset_of(step - 1, group), group)).start()

    @pl.loop(0, count)
    def _(n):
        back[me, n] = result[me, n]

    @pl.loop(0, group - 1)
    def _(step):
        other = lax.rem(me + offset_of(group - 2 - step, group), group)
        home(other, other).wait_recv()

    @pl.loop(0, count)
    def _(n):
        for q in range(chunks):
            part = [back[blocks * q + m, n] for m in range(blocks)]
            for p, tile in enumerate(swap_blocks(part)):
                out[n, p, :, lanes * q : lanes * (q + 1)] = tile

    @pl.loop(0, group - 1)
    def _(step):
        target = lax.rem(me + offset_of(step, group), group)
        forth(me, target).wait_send()
        home(me, target).wait_send()


def solution(mesh):
    group, space = mesh.shape["chaos"], mesh.shape["space"]

    def shards(kl_fields, labels, region_scale, background, galerkin_table, triple_values, direction):
        terms, fields, planes, rows, columns = direction.shape
        modes, regions = kl_fields.shape[0], region_scale.shape[0]
        width = columns // group
        lanes = planes * width
        count = terms * fields
        all_terms = terms * group
        per_term = galerkin_table.shape[0] // all_terms
        dims = (group, space, terms, fields, planes, width, modes, regions, per_term)
        table = galerkin_table[:, 1:].T
        vmem = pl.BlockSpec(memory_space=pltpu.VMEM)
        smem = pl.BlockSpec(memory_space=pltpu.SMEM)
        f32 = jnp.float32
        out = pl.pallas_call(
            functools.partial(kernel, dims),
            out_shape=jax.ShapeDtypeStruct((count, planes, rows, columns), f32),
            in_specs=[vmem] * 4 + [smem] * 3,
            out_specs=vmem,
            scratch_shapes=[
                pltpu.VMEM((group, count + 1, rows, lanes), f32),
                pltpu.VMEM((group, count + 1, rows, lanes), f32),
                pltpu.VMEM((group, count, rows, lanes), f32),
                pltpu.VMEM((group, count, rows, lanes), f32),
                pltpu.VMEM((group, modes + 1, rows, lanes), f32),
                pltpu.VMEM((group, rows, lanes), jnp.int32),
                pltpu.VMEM((3, modes + 1, rows, lanes), f32),
                pltpu.VMEM((4, modes + 1, 1, lanes), f32),
                pltpu.VMEM((4, group * count, 1, lanes), f32),
                pltpu.VMEM((modes, FACES + 1, rows, lanes), f32),
                pltpu.VMEM((FACES, rows, lanes), f32),
                pltpu.VMEM((all_terms, 3 * FACES + 1, rows, lanes), f32),
                pltpu.SemaphoreType.DMA((group,)),
                pltpu.SemaphoreType.DMA((group,)),
                pltpu.SemaphoreType.DMA((group,)),
                pltpu.SemaphoreType.DMA((group,)),
                pltpu.SemaphoreType.DMA((2, 2)),
                pltpu.SemaphoreType.DMA((2, 2)),
            ],
            compiler_params=pltpu.CompilerParams(
                collective_id=0, has_side_effects=True, vmem_limit_bytes=40 << 20
            ),
        )(
            kl_fields,
            labels,
            background,
            direction.reshape(count, planes, rows, columns),
            region_scale,
            table,
            triple_values,
        )
        return out.reshape(direction.shape)

    return jax.shard_map(
        shards,
        mesh=mesh,
        in_specs=(
            P(None, None, "space", None),
            P(None, "space", None),
            P(),
            P(None, "space", None),
            P(),
            P(),
            P("chaos", None, None, "space", None),
        ),
        out_specs=P("chaos", None, None, "space", None),
        check_vma=False,
    )
```

time: 425 us -> 47.9 us (0.11)
  the two profiles are of different devices: /device:TPU:2 before, /device:TPU:0 now
where the time goes in v1:
time: 47.9 us; the launch traced here: 47.6 us
  Pallas kernels  42.2 us (88%)
  local copies, waits for them, and re-layouts  5.35 us (11%)
    pallas_call x1, Pallas kernels, shards(): pl.pallas_call(functools.partial(kernel, dims), out_shape=jax.ShapeDtypeS...  42.2 us
    unnamed x13, local copies, waits for them, and re-layouts  4.63 us

profile of v1, /device:TPU:0, one launch (start us, length us, event | category | flops | bytes accessed | tf_op | source)
XLA Modules:
  0.0 47.6 jit_solution(15616042782830311238)
XLA Ops:
  0.0 0.0 copy-start.4
  0.0 0.0 copy-start.5
  0.0 0.7 %slice_bitcast_fusion.table = s32[2,384]{1,0:T(2,128)S(1)} fusion(s32[384,3]{0,1:T(4,128)} %param.11), kind=kLoop, calls=%fused_computation | loop fusion | bytes 6144 | tf_op jit(solution)/shard_map/transpose | solution.py:368
  0.7 0.0 copy-done.4
  0.7 0.0 copy-done.5
  0.7 0.0 copy-start
  0.7 1.1 %copy-done = f32[9,4,8,512]{3,2,1,0:T(8,128)S(1)} copy-done((f32[9,4,8,512]{3,2,1,0:T(8,128)S(1)}, f32[9,4,8,512]{3,2,1,0:T(8,128)}, u32[]{:S(2)}) %copy-start) | copy-done | bytes 589848
  1.8 0.0 copy-start.1
  1.8 1.1 %copy-done.1 = f32[3,3,4,8,512]{4,3,2,1,0:T(8,128)S(1)} copy-done((f32[3,3,4,8,512]{4,3,2,1,0:T(8,128)S(1)}, f32[3,3,4,8,512]{4,3,2,1,0:T(8,128)}, u32[]{:S(2)}) %copy-start.1) | copy-done | bytes 589848
  2.9 0.0 copy-start.2
  2.9 0.8 %copy-done.2 = s32[4,8,512]{2,1,0:T(8,128)S(1)} copy-done((s32[4,8,512]{2,1,0:T(8,128)S(1)}, s32[4,8,512]{2,1,0:T(8,128)}, u32[]{:S(2)}) %copy-start.2) | copy-done | bytes 65560
  3.7 0.0 copy-start.3
  3.7 0.8 %copy-done.3 = f32[4,8,512]{2,1,0:T(8,128)S(1)} copy-done((f32[4,8,512]{2,1,0:T(8,128)S(1)}, f32[4,8,512]{2,1,0:T(8,128)}, u32[]{:S(2)}) %copy-start.3) | copy-done | bytes 65560
  4.5 42.2 %shard_map.73 = f32[9,4,8,512]{3,2,1,0:T(8,128)S(1)} custom-call(f32[9,4,8,512]{3,2,1,0:T(8,128)S(1)} %copy-done, s32[4,8,512]{2,1,0:T(8,128)S(1)} %copy-done.2, f32[4,8,512]{2,1,0:T(8,128)S(1)} %copy-done.3, f32[9,4,8,512]{3,2,1,0:T(8,128)S(1)} %bitcast.5, f32[4,9]{1,0:T(4,128)S(1)} %copy-done.4, s32[2,384]{1,0:T(2,128)S(1)} %slice_bitcast_fusion.table, ...), custom_call_target="tpu_custom_call" | custom-call | tf_op jit(solution)/shard_map/pallas_call | solution.py:372
  46.7 0.8 %copy.9 = f32[3,3,4,8,512]{4,3,2,1,0:T(8,128)} copy(f32[3,3,4,8,512]{4,3,2,1,0:T(8,128)S(1)} %bitcast.4) | data formatting | bytes 1179648
Async XLA Ops:
  0.0 0.7 %copy-start.4 = (f32[4,9]{1,0:T(4,128)S(1)}, f32[4,9]{1,0:T(4,128)}, u32[]{:S(2)}) copy-start(f32[4,9]{1,0:T(4,128)} %scale.1) | copy-start | bytes 436
  0.0 0.7 %copy-start.5 = (f32[384]{0:T(512)S(1)}, f32[384]{0:T(512)}, u32[]{:S(2)}) copy-start(f32[384]{0:T(512)} %values.1) | copy-start | bytes 4612
  0.7 1.1 %copy-start = (f32[9,4,8,512]{3,2,1,0:T(8,128)S(1)}, f32[9,4,8,512]{3,2,1,0:T(8,128)}, u32[]{:S(2)}) copy-start(f32[9,4,8,512]{3,2,1,0:T(8,128)} %kl.1) | copy-start | bytes 1769476
  1.8 1.1 %copy-start.1 = (f32[3,3,4,8,512]{4,3,2,1,0:T(8,128)S(1)}, f32[3,3,4,8,512]{4,3,2,1,0:T(8,128)}, u32[]{:S(2)}) copy-start(f32[3,3,4,8,512]{4,3,2,1,0:T(8,128)} %param.13) | copy-start | bytes 1769476
  2.9 0.8 %copy-start.2 = (s32[4,8,512]{2,1,0:T(8,128)S(1)}, s32[4,8,512]{2,1,0:T(8,128)}, u32[]{:S(2)}) copy-start(s32[4,8,512]{2,1,0:T(8,128)} %labels.1) | copy-start | bytes 196612
  3.7 0.8 %copy-start.3 = (f32[4,8,512]{2,1,0:T(8,128)S(1)}, f32[4,8,512]{2,1,0:T(8,128)}, u32[]{:S(2)}) copy-start(f32[4,8,512]{2,1,0:T(8,128)} %background.1) | copy-start | bytes 196612

commit v2 on v1

v2 whole, which is shorter than its diff:
```python
import functools
import math

import jax
import jax.numpy as jnp
from jax import lax
from jax.experimental import pallas as pl
from jax.experimental.pallas import tpu as pltpu
from jax.sharding import PartitionSpec as P

MESH = pl.DeviceIdType.MESH
FACES = 6
VMEM_BYTES = 67043328


def peer_of(me, step, group):
    half = group // 2
    mine = half * (me // half)
    cross = half - mine + (me + step) % half
    near = mine + (me + step + 1) % half
    return jnp.where(step < half, cross, near)


def kernel(
    dims,
    kl_hbm,
    labels_hbm,
    background_hbm,
    direction_hbm,
    scale_hbm,
    table_hbm,
    values_hbm,
    out,
    kl,
    labels,
    background,
    direction,
    scale,
    table,
    values,
    send,
    recv,
    result,
    back,
    kl_tiles,
    label_tiles,
    coef,
    coef_halo,
    row_halo,
    column_halo,
    conduct,
    drift,
    flux,
    centre,
    load_sem,
    send_sem,
    recv_sem,
    back_send_sem,
    back_recv_sem,
    row_send_sem,
    row_recv_sem,
    column_send_sem,
    column_recv_sem,
):
    group, space, terms, fields, planes, width, modes, regions, per_term, packed = dims
    rows = direction.shape[2]
    lanes = planes * width
    blocks = lanes // width
    chunks = group // blocks
    all_terms = group * terms
    me = lax.axis_index("chaos")
    here = lax.axis_index("space")

    loads = [
        pltpu.make_async_copy(source, target, load_sem.at[n])
        for n, (source, target) in enumerate(
            (
                (direction_hbm, direction),
                (kl_hbm, kl),
                (labels_hbm, labels),
                (background_hbm, background),
                (scale_hbm, scale),
                (table_hbm, table),
                (values_hbm, values),
            )
        )
    ]
    for load in loads:
        load.start()

    barrier = pltpu.get_barrier_semaphore()
    for g in range(1, group):
        pl.semaphore_signal(
            barrier, inc=1, device_id={"chaos": lax.rem(me + g, group)}, device_id_type=MESH
        )

    @pl.when(here > 0)
    def _():
        pl.semaphore_signal(barrier, inc=1, device_id={"space": here - 1}, device_id_type=MESH)

    @pl.when(here < space - 1)
    def _():
        pl.semaphore_signal(barrier, inc=1, device_id={"space": here + 1}, device_id_type=MESH)

    lane = lax.broadcasted_iota(jnp.int32, (rows, lanes), 1)
    row = lax.broadcasted_iota(jnp.int32, (rows, lanes), 0)
    column = lane % width
    plane = lane // width

    def turn(tile, shift, axis=1):
        shift = shift % tile.shape[axis]
        return tile if shift == 0 else pltpu.roll(tile, shift, axis)

    def swap_blocks(tiles):
        swapped = []
        for m in range(blocks):
            tile = tiles[0] if m == 0 else turn(tiles[0], -width * m)
            for p in range(1, blocks):
                tile = jnp.where(plane == p, turn(tiles[p], width * (p - m)), tile)
            swapped.append(tile)
        return swapped

    loads[0].wait()

    @pl.loop(0, fields)
    def _(f):
        for t in range(terms):
            for q in range(chunks):
                part = [
                    direction[t * fields + f, p, :, lanes * q : lanes * (q + 1)]
                    for p in range(planes)
                ]
                for m, tile in enumerate(swap_blocks(part)):
                    send[f, blocks * q + m, t] = tile

    beside = jnp.minimum(here, 1) + jnp.minimum(space - 1 - here, 1)
    pl.semaphore_wait(barrier, group - 1 + beside)

    def forth(f, source, target):
        return pltpu.make_async_remote_copy(
            src_ref=send.at[f, target],
            dst_ref=recv.at[f, source],
            send_sem=send_sem.at[f, target],
            recv_sem=recv_sem.at[f, source],
            device_id={"chaos": target},
            device_id_type=MESH,
        )

    for f in range(fields):

        @pl.loop(0, group - 1)
        def _(step):
            forth(f, me, peer_of(me, step, group)).start()

        for t in range(terms):
            recv[f, me, t] = send[f, me, t]

    for load in loads[1:]:
        load.wait()

    @pl.loop(0, modes)
    def _(k):
        for q in range(chunks):
            part = [kl[k, p, :, lanes * q : lanes * (q + 1)] for p in range(planes)]
            for m, tile in enumerate(swap_blocks(part)):
                kl_tiles[blocks * q + m, k] = tile

    for q in range(chunks):
        part = [background[p, :, lanes * q : lanes * (q + 1)] for p in range(planes)]
        for m, tile in enumerate(swap_blocks(part)):
            kl_tiles[blocks * q + m, modes] = tile
        part = [labels[p, :, lanes * q : lanes * (q + 1)] for p in range(planes)]
        for m, tile in enumerate(swap_blocks(part)):
            label_tiles[blocks * q + m] = tile

    places = (me, jnp.minimum(me + 1, group - 1), jnp.maximum(me - 1, 0))
    inside = (None, me < group - 1, me > 0)
    for slot, (place, ok) in enumerate(zip(places, inside)):
        region_tile = label_tiles[place]
        for k in range(modes):
            lookup = jnp.full((rows, lanes), scale[0, k])
            for region in range(1, regions):
                lookup = jnp.where(region_tile == region, scale[region, k], lookup)
            tile = kl_tiles[place, k] * lookup
            coef[slot, k] = tile if ok is None else jnp.where(ok, tile, 0.0)
        tile = kl_tiles[place, modes]
        coef[slot, modes] = tile if ok is None else jnp.where(ok, tile, 0.0)

    def exchange(buffer, axis, position, size, send_sems, recv_sems):
        def copy(way):
            return pltpu.make_async_remote_copy(
                src_ref=buffer.at[way],
                dst_ref=buffer.at[2 + way],
                send_sem=send_sems.at[way],
                recv_sem=recv_sems.at[way],
                device_id={axis: position + 1 - 2 * way},
                device_id_type=MESH,
            )

        def start():
            @pl.when(position < size - 1)
            def _():
                copy(0).start()

            @pl.when(position > 0)
            def _():
                copy(1).start()

        def finish():
            @pl.when(position > 0)
            def _():
                copy(0).wait_recv()

            @pl.when(position < size - 1)
            def _():
                copy(1).wait_recv()

            @pl.when(position == 0)
            def _():
                buffer[2] = jnp.zeros(buffer.shape[1:], jnp.float32)

            @pl.when(position == size - 1)
            def _():
                buffer[3] = jnp.zeros(buffer.shape[1:], jnp.float32)

            @pl.when(position < size - 1)
            def _():
                copy(0).wait_send()

            @pl.when(position > 0)
            def _():
                copy(1).wait_send()

        return start, finish

    def side_neighbours(tile, before, after):
        return (
            jnp.where(plane < planes - 1, turn(tile, -width), 0.0),
            jnp.where(plane > 0, turn(tile, width), 0.0),
            jnp.where(column == width - 1, after, turn(tile, -1)),
            jnp.where(column == 0, before, turn(tile, 1)),
        )

    def row_neighbours(tile, above, below):
        return (
            jnp.where(row == rows - 1, jnp.broadcast_to(below, tile.shape), turn(tile, -1, 0)),
            jnp.where(row == 0, jnp.broadcast_to(above, tile.shape), turn(tile, 1, 0)),
        )

    for k in range(modes + 1):
        coef_halo[0, k] = coef[0, k, rows - 1 : rows, :]
        coef_halo[1, k] = coef[0, k, 0:1, :]

    start_coef, finish_coef = exchange(
        coef_halo, "space", here, space, row_send_sem.at[fields], row_recv_sem.at[fields]
    )
    start_coef()
    finish_coef()
    for k in range(modes + 1):
        tile = coef[0, k]
        others = row_neighbours(tile, coef_halo[2, k], coef_halo[3, k]) + side_neighbours(
            tile, turn(coef[2, k], 1 - width), turn(coef[1, k], width - 1)
        )
        for face, other in enumerate(others):
            if k < modes:
                conduct[k, face] = 0.5 * (tile + other)
            else:
                drift[face] = 0.5 * (other - tile)
        if k < modes:
            conduct[k, FACES] = tile

    def home(f, source, target):
        return pltpu.make_async_remote_copy(
            src_ref=result.at[f, target],
            dst_ref=back.at[f, source],
            send_sem=back_send_sem.at[f, target],
            recv_sem=back_recv_sem.at[f, source],
            device_id={"chaos": target},
            device_id_type=MESH,
        )

    def gather_field(f):
        @pl.loop(0, group)
        def _(step):
            source = peer_of(me, step, group)

            @pl.when(step < group - 1)
            def _():
                forth(f, source, source).wait_recv()

            for t in range(terms):
                tile = recv[f, source, t]
                row_halo[f, 0, source * terms + t] = tile[rows - 1 : rows]
                row_halo[f, 1, source * terms + t] = tile[0:1]

        start_rows, finish_rows = exchange(
            row_halo.at[f], "space", here, space, row_send_sem.at[f], row_recv_sem.at[f]
        )
        start_rows()

        @pl.loop(0, all_terms // packed)
        def _(g):
            last = jnp.zeros((rows, lanes), jnp.float32)
            first = jnp.zeros((rows, lanes), jnp.float32)
            for n in range(packed):
                j = g * packed + n
                tile = recv[f, j // terms, j % terms]
                last = jnp.where(column == n, turn(tile, n - (width - 1)), last)
                first = jnp.where(column == n, turn(tile, n), first)
            column_halo[f, 0, g] = last
            column_halo[f, 1, g] = first

        start_columns, finish_columns = exchange(
            column_halo.at[f], "chaos", me, group, column_send_sem.at[f], column_recv_sem.at[f]
        )
        start_columns()
        finish_rows()
        finish_columns()

    def flux_of(f):
        @pl.loop(0, all_terms // packed)
        def _(g):
            before, after = column_halo[f, 2, g], column_halo[f, 3, g]
            for n in range(packed):
                j = g * packed + n
                tile = recv[f, j // terms, j % terms]
                others = row_neighbours(
                    tile, row_halo[f, 2, j], row_halo[f, 3, j]
                ) + side_neighbours(tile, turn(before, -n), turn(after, width - 1 - n))
                for face, other in enumerate(others):
                    if f == 0:
                        flux[0, j, face] = tile - other
                    elif f == 1:
                        flux[1, j, face] = (
                            (tile - other) - drift[face] * (tile + other) + flux[0, j, face]
                        )
                    else:
                        flux[2, j, face] = (
                            (tile - other) + drift[face] * (tile + other) - flux[0, j, face]
                        )
                if f == 2:
                    centre[j] = recv[1, j // terms, j % terms] - tile

    def apply(which):
        def send_home(step):
            for f in which:
                home(f, me, peer_of(me, step, group)).start()

        @pl.loop(0, group)
        def _(step):
            target = peer_of(me, step, group)
            for t in range(terms):
                total = {f: jnp.zeros((rows, lanes), jnp.float32) for f in which}
                for e in range(per_term):
                    entry = (target * terms + t) * per_term + e
                    j, k, value = table[1, entry], table[2, entry], values[entry]
                    if 0 in which:
                        total[0] += (value * conduct[k, FACES]) * centre[j]
                    for face in range(FACES):
                        h = value * conduct[k, face]
                        for f in which:
                            total[f] += h * flux[f, j, face]
                for f in which:
                    result[f, target, t] = total[f]

            @pl.when(step > 0)
            def _():
                send_home(step - 1)

        for f in which:
            for t in range(terms):
                back[f, me, t] = result[f, me, t]

    def place_field(f):
        @pl.loop(0, group - 1)
        def _(step):
            other = peer_of(me, step, group)
            home(f, other, other).wait_recv()

        @pl.loop(0, terms)
        def _(t):
            for q in range(chunks):
                part = [back[f, blocks * q + m, t] for m in range(blocks)]
                for p, tile in enumerate(swap_blocks(part)):
                    out[t * fields + f, p, :, lanes * q : lanes * (q + 1)] = tile

    gather_field(0)
    flux_of(0)
    gather_field(1)
    flux_of(1)
    apply((1,))
    gather_field(2)
    flux_of(2)
    apply((0, 2))
    for f in (1, 0, 2):
        place_field(f)

    @pl.loop(0, group - 1)
    def _(step):
        target = peer_of(me, step, group)
        for f in range(fields):
            forth(f, me, target).wait_send()
            home(f, me, target).wait_send()


def solution(mesh):
    group, space = mesh.shape["chaos"], mesh.shape["space"]

    def shards(kl_fields, labels, region_scale, background, galerkin_table, triple_values, direction):
        terms, fields, planes, rows, columns = direction.shape
        modes, regions = kl_fields.shape[0], region_scale.shape[0]
        width = columns // group
        lanes = planes * width
        count = terms * fields
        all_terms = terms * group
        per_term = galerkin_table.shape[0] // all_terms
        packed = math.gcd(all_terms, width)
        dims = (group, space, terms, fields, planes, width, modes, regions, per_term, packed)
        table = galerkin_table.T
        hbm = pl.BlockSpec(memory_space=pltpu.HBM)
        f32 = jnp.float32
        tile = (rows, lanes)
        dma = pltpu.SemaphoreType.DMA
        out = pl.pallas_call(
            functools.partial(kernel, dims),
            out_shape=jax.ShapeDtypeStruct((count, planes, rows, columns), f32),
            in_specs=[hbm] * 7,
            out_specs=pl.BlockSpec(memory_space=pltpu.VMEM),
            scratch_shapes=[
                pltpu.VMEM(kl_fields.shape, f32),
                pltpu.VMEM(labels.shape, jnp.int32),
                pltpu.VMEM(background.shape, f32),
                pltpu.VMEM((count, planes, rows, columns), f32),
                pltpu.SMEM(region_scale.shape, f32),
                pltpu.SMEM(table.shape, jnp.int32),
                pltpu.SMEM(triple_values.shape, f32),
                pltpu.VMEM((fields, group, terms) + tile, f32),
                pltpu.VMEM((fields, group, terms) + tile, f32),
                pltpu.VMEM((fields, group, terms) + tile, f32),
                pltpu.VMEM((fields, group, terms) + tile, f32),
                pltpu.VMEM((group, modes + 1) + tile, f32),
                pltpu.VMEM((group,) + tile, jnp.int32),
                pltpu.VMEM((3, modes + 1) + tile, f32),
                pltpu.VMEM((4, modes + 1, 1, lanes), f32),
                pltpu.VMEM((fields, 4, all_terms, 1, lanes), f32),
                pltpu.VMEM((fields, 4, all_terms // packed) + tile, f32),
                pltpu.VMEM((modes, FACES + 1) + tile, f32),
                pltpu.VMEM((FACES,) + tile, f32),
                pltpu.VMEM((fields, all_terms, FACES) + tile, f32),
                pltpu.VMEM((all_terms,) + tile, f32),
                dma((7,)),
                dma((fields, group)),
                dma((fields, group)),
                dma((fields, group)),
                dma((fields, group)),
                dma((fields + 1, 2)),
                dma((fields + 1, 2)),
                dma((fields, 2)),
                dma((fields, 2)),
            ],
            compiler_params=pltpu.CompilerParams(
                collective_id=0, has_side_effects=True, vmem_limit_bytes=VMEM_BYTES
            ),
        )(
            kl_fields,
            labels,
            background,
            direction.reshape(count, planes, rows, columns),
            region_scale,
            table,
            triple_values,
        )
        return out.reshape(direction.shape)

    return jax.shard_map(
        shards,
        mesh=mesh,
        in_specs=(
            P(None, None, "space", None),
            P(None, "space", None),
            P(),
            P(None, "space", None),
            P(),
            P(),
            P("chaos", None, None, "space", None),
        ),
        out_specs=P("chaos", None, None, "space", None),
        check_vma=False,
    )
```

time: 47.9 us -> 46.4 us (0.969)
  local copies, waits for them, and re-layouts: 5.35 us -> 1.92 us
  Pallas kernels: 42.2 us -> 44.3 us
    unnamed x13 -> x1, local copies, waits for them, and re-layouts: 4.63 us -> 1.92 us
    pallas_call x1, Pallas kernels: 42.2 us -> 44.3 us  [shards(): pl.pallas_call(functools.partial(kernel, dims), out_shape=jax.ShapeDtypeS...]
    transpose x1 -> x0, local copies, waits for them, and re-layouts: 0.72 us -> none  [shards(): table = galerkin_table[:, 1:].T]
where the time goes in v2:
time: 46.4 us; the launch traced here: 46.2 us
  Pallas kernels  44.3 us (95%)
  local copies, waits for them, and re-layouts  1.92 us (4%)
    pallas_call x1, Pallas kernels, shards(): pl.pallas_call(functools.partial(kernel, dims), out_shape=jax.ShapeDtypeS...  44.3 us
    unnamed x1, local copies, waits for them, and re-layouts  1.92 us

profile of v2, /device:TPU:0, one launch (start us, length us, event | category | flops | bytes accessed | tf_op | source)
XLA Modules:
  0.0 46.2 jit_solution(18053904439433898333)
XLA Ops:
  0.0 44.3 %shard_map.73 = f32[9,4,8,512]{3,2,1,0:T(8,128)} custom-call(f32[9,4,8,512]{3,2,1,0:T(8,128)} %kl_hbm.1, s32[4,8,512]{2,1,0:T(8,128)} %labels_hbm.1, f32[4,8,512]{2,1,0:T(8,128)} %background_hbm.1, f32[9,4,8,512]{3,2,1,0:T(8,128)} %bitcast.4, f32[4,9]{1,0:T(4,128)} %scale_hbm.1, s32[3,384]{1,0:T(4,128)} %bitcast.5, f32[384]{0:T(512)} %values_hbm.1), custom_call_target="tpu_custom_call" | custom-call | tf_op jit(solution)/shard_map/pallas_call | solution.py:424
  44.3 1.9 %copy.9 = f32[3,3,4,8,512]{4,3,2,1,0:T(8,128)} copy(f32[3,3,4,8,512]{4,3,2,1,0:T(8,128)} %bitcast.3) | data formatting | bytes 1179648

commit v3 on v2

--- a/solution.py
+++ b/solution.py
@@ -1,5 +1,4 @@
 import functools
-import math
 
 import jax
 import jax.numpy as jnp
@@ -10,7 +9,7 @@
 
 MESH = pl.DeviceIdType.MESH
 FACES = 6
-VMEM_BYTES = 67043328
+VMEM_BYTES = 40 << 20
 
 
 def peer_of(me, step, group):
@@ -47,7 +46,6 @@
     coef,
     coef_halo,
     row_halo,
-    column_halo,
     conduct,
     drift,
     flux,
@@ -59,15 +57,12 @@
     back_recv_sem,
     row_send_sem,
     row_recv_sem,
-    column_send_sem,
-    column_recv_sem,
 ):
-    group, space, terms, fields, planes, width, modes, regions, per_term, packed = dims
+    group, space, terms, fields, planes, width, modes, regions, per_term = dims
     rows = direction.shape[2]
     lanes = planes * width
     blocks = lanes // width
     chunks = group // blocks
-    all_terms = group * terms
     me = lax.axis_index("chaos")
     here = lax.axis_index("space")
 
@@ -133,13 +128,33 @@
                 for m, tile in enumerate(swap_blocks(part)):
                     send[f, blocks * q + m, t] = tile
 
+    half = width // 2
+
+    @pl.loop(0, group)
+    def _(d):
+        after = jnp.minimum(d + 1, group - 1)
+        before = jnp.maximum(d - 1, 0)
+        right = jnp.zeros((rows, lanes), jnp.float32)
+        left = jnp.zeros((rows, lanes), jnp.float32)
+        for f in range(fields):
+            for t in range(terms):
+                n = f * terms + t
+                right = jnp.where(column == n, turn(send[f, after, t], n), right)
+                left = jnp.where(
+                    column == half + n, turn(send[f, before, t], half + n - (width - 1)), left
+                )
+        right = jnp.where(d < group - 1, right, 0.0)
+        left = jnp.where(d > 0, left, 0.0)
+        send[0, d, terms] = jnp.where(column < half, right, left)
+
     beside = jnp.minimum(here, 1) + jnp.minimum(space - 1 - here, 1)
     pl.semaphore_wait(barrier, group - 1 + beside)
 
     def forth(f, source, target):
+        size = terms + 1 if f == 0 else terms
         return pltpu.make_async_remote_copy(
-            src_ref=send.at[f, target],
-            dst_ref=recv.at[f, source],
+            src_ref=send.at[f, target, pl.ds(0, size)],
+            dst_ref=recv.at[f, source, pl.ds(0, size)],
             send_sem=send_sem.at[f, target],
             recv_sem=recv_sem.at[f, source],
             device_id={"chaos": target},
@@ -152,7 +167,7 @@
         def _(step):
             forth(f, me, peer_of(me, step, group)).start()
 
-        for t in range(terms):
+        for t in range(terms + 1 if f == 0 else terms):
             recv[f, me, t] = send[f, me, t]
 
     for load in loads[1:]:
@@ -255,19 +270,28 @@
         coef_halo, "space", here, space, row_send_sem.at[fields], row_recv_sem.at[fields]
     )
     start_coef()
+
+    def store_coef(k, face, tile, other):
+        if k < modes:
+            conduct[k, face] = 0.5 * (tile + other)
+        else:
+            drift[face] = 0.5 * (other - tile)
+
+    for k in range(modes + 1):
+        tile = coef[0, k]
+        others = side_neighbours(
+            tile, turn(coef[2, k], 1 - width), turn(coef[1, k], width - 1)
+        )
+        for face, other in enumerate(others):
+            store_coef(k, 2 + face, tile, other)
+        if k < modes:
+            conduct[k, FACES] = tile
+
     finish_coef()
     for k in range(modes + 1):
         tile = coef[0, k]
-        others = row_neighbours(tile, coef_halo[2, k], coef_halo[3, k]) + side_neighbours(
-            tile, turn(coef[2, k], 1 - width), turn(coef[1, k], width - 1)
-        )
-        for face, other in enumerate(others):
-            if k < modes:
-                conduct[k, face] = 0.5 * (tile + other)
-            else:
-                drift[face] = 0.5 * (other - tile)
-        if k < modes:
-            conduct[k, FACES] = tile
+        for face, other in enumerate(row_neighbours(tile, coef_halo[2, k], coef_halo[3, k])):
+            store_coef(k, face, tile, other)
 
     def home(f, source, target):
         return pltpu.make_async_remote_copy(
@@ -297,49 +321,41 @@
             row_halo.at[f], "space", here, space, row_send_sem.at[f], row_recv_sem.at[f]
         )
         start_rows()
-
-        @pl.loop(0, all_terms // packed)
-        def _(g):
-            last = jnp.zeros((rows, lanes), jnp.float32)
-            first = jnp.zeros((rows, lanes), jnp.float32)
-            for n in range(packed):
-                j = g * packed + n
-                tile = recv[f, j // terms, j % terms]
-                last = jnp.where(column == n, turn(tile, n - (width - 1)), last)
-                first = jnp.where(column == n, turn(tile, n), first)
-            column_halo[f, 0, g] = last
-            column_halo[f, 1, g] = first
-
-        start_columns, finish_columns = exchange(
-            column_halo.at[f], "chaos", me, group, column_send_sem.at[f], column_recv_sem.at[f]
-        )
-        start_columns()
-        finish_rows()
-        finish_columns()
-
-    def flux_of(f):
-        @pl.loop(0, all_terms // packed)
-        def _(g):
-            before, after = column_halo[f, 2, g], column_halo[f, 3, g]
-            for n in range(packed):
-                j = g * packed + n
-                tile = recv[f, j // terms, j % terms]
-                others = row_neighbours(
-                    tile, row_halo[f, 2, j], row_halo[f, 3, j]
-                ) + side_neighbours(tile, turn(before, -n), turn(after, width - 1 - n))
+        return finish_rows
+
+    def store_flux(f, j, face, tile, other):
+        if f == 0:
+            flux[0, j, face] = tile - other
+        elif f == 1:
+            flux[1, j, face] = (tile - other) - drift[face] * (tile + other) + flux[0, j, face]
+        else:
+            flux[2, j, face] = (tile - other) + drift[face] * (tile + other) - flux[0, j, face]
+
+    def side_flux(f):
+        @pl.loop(0, group)
+        def _(source):
+            rim = recv[0, source, terms]
+            for t in range(terms):
+                n = f * terms + t
+                j = source * terms + t
+                tile = recv[f, source, t]
+                others = side_neighbours(
+                    tile, turn(rim, -half - n), turn(rim, width - 1 - n)
+                )
                 for face, other in enumerate(others):
-                    if f == 0:
-                        flux[0, j, face] = tile - other
-                    elif f == 1:
-                        flux[1, j, face] = (
-                            (tile - other) - drift[face] * (tile + other) + flux[0, j, face]
-                        )
-                    else:
-                        flux[2, j, face] = (
-                            (tile - other) + drift[face] * (tile + other) - flux[0, j, face]
-                        )
+                    store_flux(f, j, 2 + face, tile, other)
                 if f == 2:
-                    centre[j] = recv[1, j // terms, j % terms] - tile
+                    centre[j] = recv[1, source, t] - tile
+
+    def row_flux(f):
+        @pl.loop(0, group)
+        def _(source):
+            for t in range(terms):
+                j = source * terms + t
+                tile = recv[f, source, t]
+                others = row_neighbours(tile, row_halo[f, 2, j], row_halo[f, 3, j])
+                for face, other in enumerate(others):
+                    store_flux(f, j, face, tile, other)
 
     def apply(which):
         def send_home(step):
@@ -384,13 +400,19 @@
                 for p, tile in enumerate(swap_blocks(part)):
                     out[t * fields + f, p, :, lanes * q : lanes * (q + 1)] = tile
 
-    gather_field(0)
-    flux_of(0)
-    gather_field(1)
-    flux_of(1)
+    finish_rows = gather_field(0)
+    side_flux(0)
+    finish_rows()
+    row_flux(0)
+    finish_rows = gather_field(1)
+    side_flux(1)
+    finish_rows()
+    row_flux(1)
     apply((1,))
-    gather_field(2)
-    flux_of(2)
+    finish_rows = gather_field(2)
+    side_flux(2)
+    finish_rows()
+    row_flux(2)
     apply((0, 2))
     for f in (1, 0, 2):
         place_field(f)
@@ -414,8 +436,7 @@
         count = terms * fields
         all_terms = terms * group
         per_term = galerkin_table.shape[0] // all_terms
-        packed = math.gcd(all_terms, width)
-        dims = (group, space, terms, fields, planes, width, modes, regions, per_term, packed)
+        dims = (group, space, terms, fields, planes, width, modes, regions, per_term)
         table = galerkin_table.T
         hbm = pl.BlockSpec(memory_space=pltpu.HBM)
         f32 = jnp.float32
@@ -434,8 +455,8 @@
                 pltpu.SMEM(region_scale.shape, f32),
                 pltpu.SMEM(table.shape, jnp.int32),
                 pltpu.SMEM(triple_values.shape, f32),
-                pltpu.VMEM((fields, group, terms) + tile, f32),
-                pltpu.VMEM((fields, group, terms) + tile, f32),
+                pltpu.VMEM((fields, group, terms + 1) + tile, f32),
+                pltpu.VMEM((fields, group, terms + 1) + tile, f32),
                 pltpu.VMEM((fields, group, terms) + tile, f32),
                 pltpu.VMEM((fields, group, terms) + tile, f32),
                 pltpu.VMEM((group, modes + 1) + tile, f32),
@@ -443,7 +464,6 @@
                 pltpu.VMEM((3, modes + 1) + tile, f32),
                 pltpu.VMEM((4, modes + 1, 1, lanes), f32),
                 pltpu.VMEM((fields, 4, all_terms, 1, lanes), f32),
-                pltpu.VMEM((fields, 4, all_terms // packed) + tile, f32),
                 pltpu.VMEM((modes, FACES + 1) + tile, f32),
                 pltpu.VMEM((FACES,) + tile, f32),
                 pltpu.VMEM((fields, all_terms, FACES) + tile, f32),
@@ -455,20 +475,23 @@
                 dma((fields, group)),
                 dma((fields + 1, 2)),
                 dma((fields + 1, 2)),
-                dma((fields, 2)),
-                dma((fields, 2)),
             ],
             compiler_params=pltpu.CompilerParams(
                 collective_id=0, has_side_effects=True, vmem_limit_bytes=VMEM_BYTES
             ),
         )(
-            kl_fields,
-            labels,
-            background,
-            direction.reshape(count, planes, rows, columns),
-            region_scale,
-            table,
-            triple_values,
+            *(
+                pltpu.with_memory_space_constraint(x, pltpu.HBM)
+                for x in (
+                    kl_fields,
+                    labels,
+                    background,
+                    direction.reshape(count, planes, rows, columns),
+                    region_scale,
+                    table,
+                    triple_values,
+                )
+            )
         )
         return out.reshape(direction.shape)
 

time: 46.4 us -> 42.5 us (0.916)
  Pallas kernels: 44.3 us -> 41.6 us
  local copies, waits for them, and re-layouts: 1.92 us -> 0.82 us
    pallas_call x1, Pallas kernels: 44.3 us -> 41.6 us  [shards(): pl.pallas_call(functools.partial(kernel, dims), out_shape=jax.ShapeDtypeS...]
    unnamed x1, local copies, waits for them, and re-layouts: 1.92 us -> 0.82 us
where the time goes in v3:
time: 42.5 us; the launch traced here: 42.4 us
  Pallas kernels  41.6 us (98%)
  local copies, waits for them, and re-layouts  0.82 us (2%)
    pallas_call x1, Pallas kernels, shards(): pl.pallas_call(functools.partial(kernel, dims), out_shape=jax.ShapeDtypeS...  41.6 us

profile of v3, /device:TPU:0, one launch (start us, length us, event | category | flops | bytes accessed | tf_op | source)
XLA Modules:
  0.0 42.4 jit_solution(4718678194814444022)
XLA Ops:
  0.0 41.6 %shard_map.73 = f32[9,4,8,512]{3,2,1,0:T(8,128)S(1)} custom-call(f32[9,4,8,512]{3,2,1,0:T(8,128)} %kl_hbm.1, s32[4,8,512]{2,1,0:T(8,128)} %labels_hbm.1, f32[4,8,512]{2,1,0:T(8,128)} %background_hbm.1, f32[9,4,8,512]{3,2,1,0:T(8,128)} %bitcast.4, f32[4,9]{1,0:T(4,128)} %scale_hbm.1, s32[3,384]{1,0:T(4,128)} %bitcast.5, f32[384]{0:T(512)} %values_hbm.1), custom_call_target="tpu_custom_call" | custom-call | tf_op jit(solution)/shard_map/pallas_call | solution.py:445
  41.6 0.8 %copy.9 = f32[3,3,4,8,512]{4,3,2,1,0:T(8,128)} copy(f32[3,3,4,8,512]{4,3,2,1,0:T(8,128)S(1)} %bitcast.3) | data formatting | bytes 1179648
